TPU v7x, 32 devices: a whole 2x2x4 slice. The times are simulated.
32 devices in a mesh: layer: 16 (over z, x, core), dp: 2 (over y).
Axes of the slice: x: 2, y: 2, z: 4, core: 2. Of those that a mesh axis runs over, the one named last changes fastest.
Arguments:
- weights: float32 [32, 1024, 1024], P('layer', 'dp'), may hold values from -6 to 6
- momentum: float32 [32, 1024, 1024], P('layer', 'dp'), may hold values from -3 to 3
- boundary: float32 [16, 512, 1024], P('layer', 'dp'), may hold values from -6 to 6
- adjoint: float32 [16, 512, 1024], P('layer', 'dp'), may hold values from -6 to 6
- target: float32 [512, 1024], P('dp'), may hold values from -6 to 6
Outputs:
- new_weights: float32 [32, 1024, 1024], P('layer', 'dp')
- new_momentum: float32 [32, 1024, 1024], P('layer', 'dp')
- new_boundary: float32 [16, 512, 1024], P('layer', 'dp')
- new_adjoint: float32 [16, 512, 1024], P('layer', 'dp')
All inputs are finite; a program needn't handle non-finite values.
Results may differ from a plain program's by a relative error of at most 0.012.
Values may be sent and summed in bfloat16 or wider, within the bound.
A program may use at most 64 MiB of HBM per device.

v0:
```python
import math

import jax
import jax.numpy as jnp
from jax import lax
from jax.sharding import PartitionSpec as P

STEPS = 2
SWEEPS = 2


step_size = 0.5
momentum_decay = 0.9
learn_rate = 0.05


def passed_along(value, axis, by):
    devices = lax.axis_size(axis)
    pairs = [(i, i + by) for i in range(devices) if 0 <= i + by < devices]
    return lax.ppermute(value, axis, pairs)


def forward_group(current, full_weights, width_scale):
    inputs_list = []
    slopes_list = []
    for layer_at in range(full_weights.shape[0]):
        rounded = current.astype(jnp.bfloat16)
        product = jnp.dot(rounded, full_weights[layer_at], preferred_element_type=jnp.float32)
        squashed = jnp.tanh(product * width_scale)
        current = current + step_size * squashed
        inputs_list.append(rounded)
        slopes_list.append(squashed)
    return (current, inputs_list, slopes_list)


def pull_back(signal, matrix):
    return lax.dot_general(
        signal, matrix, (((1,), (1,)), ((), ())), preferred_element_type=jnp.float32
    )


def backward_group(cotangent, full_weights, slopes_list, width_scale):
    for layer_at in reversed(range(len(slopes_list))):
        slope = slopes_list[layer_at]
        signal = (cotangent * (1.0 - slope * slope)).astype(jnp.bfloat16)
        cotangent = cotangent + step_size * width_scale * pull_back(signal, full_weights[layer_at])
    return cotangent


def outer_rows(left, right):
    return lax.dot_general(
        left, right, (((0,), (0,)), ((), ())), preferred_element_type=jnp.float32
    )


def local(weights, momentum, boundary, adjoint, target):
    groups = lax.axis_size("layer")
    group_at = lax.axis_index("layer")
    shards = lax.axis_size("dp")
    shard_at = lax.axis_index("dp")
    width = weights.shape[2]
    own_rows = weights.shape[1]
    width_scale = 1.0 / math.sqrt(width)
    row_scale = 1.0 / math.sqrt(boundary.shape[1] * shards)
    is_first = group_at == 0
    is_last = group_at == groups - 1
    current_in = boundary[0]
    cotangent_in = adjoint[0]
    for update_at in range(STEPS):
        full_weights = lax.all_gather(weights.astype(jnp.bfloat16), "dp", axis=1, tiled=True)
        for sweep_at in range(SWEEPS):
            outgoing = forward_group(current_in, full_weights, width_scale)[0]
            received = passed_along(outgoing, "layer", 1)
            current_in = jnp.where(is_first, current_in, received)
        finals, inputs_list, slopes_list = forward_group(current_in, full_weights, width_scale)
        missing = finals - target
        for sweep_at in range(SWEEPS):
            starting = backward_group(cotangent_in, full_weights, slopes_list, width_scale)
            received = passed_along(starting, "layer", -1)
            cotangent_in = jnp.where(is_last, missing, received)
        cotangent = cotangent_in
        grads = [None] * len(slopes_list)
        for layer_at in reversed(range(len(slopes_list))):
            slope = slopes_list[layer_at]
            signal = (cotangent * (1.0 - slope * slope)).astype(jnp.bfloat16)
            layer_input = inputs_list[layer_at]
            columns = lax.dynamic_slice_in_dim(
                lax.all_gather(layer_input, "dp", axis=0, tiled=True),
                shard_at * own_rows,
                own_rows,
                1,
            )
            summed = outer_rows(columns, lax.all_gather(signal, "dp", axis=0, tiled=True))
            grads[layer_at] = summed * row_scale
            if layer_at > 0:
                cotangent = cotangent + step_size * width_scale * pull_back(
                    signal, full_weights[layer_at]
                )
        momentum = momentum_decay * momentum + jnp.stack(grads, axis=0)
        weights = weights - learn_rate * momentum
    return (weights, momentum, current_in[None], cotangent_in[None])


def solution(mesh):
    placed = (
        P("layer", "dp", None),
        P("layer", "dp", None),
        P("layer", "dp", None),
        P("layer", "dp", None),
        P("dp", None),
    )
    return jax.shard_map(
        local,
        mesh=mesh,
        in_specs=placed,
        out_specs=(
            P("layer", "dp", None),
            P("layer", "dp", None),
            P("layer", "dp", None),
            P("layer", "dp", None),
        ),
        check_vma=False,
    )
```

profile of v0, /device:TPU:0, one launch (start us, length us, event | category | flops | bytes accessed | tf_op | source)
XLA Modules:
  0.0 482.2 jit_solution(8640510637645091248)
XLA Ops:
  7.2 3.9 convert_element_type.81
  11.2 59.6 %all-gather.11.cloned.1.call-done = bf16[2,1024,1024]{2,1,0:T(8,128)(2,1)} async-done(((bf16[2,512,1024]{2,1,0:T(8,128)(2,1)}), bf16[2,1024,1024]{2,1,0:T(8,128)(2,1)}) %all-gather.11.cloned.1.call-update) | async-done | bytes 4194320 | tf_op jit(solution)/shard_map/all_gather | solution.py:70
  78.2 2.8 fusion.34
  81.7 13.3 %collective-permute-start.1 = (f32[256,1024]{1,0:T(8,128)S(1)}, f32[256,1024]{1,0:T(8,128)S(1)}, u32[]{:S(2)}, u32[]{:S(2)}) collective-permute-start(f32[256,1024]{1,0:T(8,128)S(1)} %fusion.31), channel_id=1, source_target_pairs={{0,2},{2,4},{4,6},{6,8},{8,10},{10,12},{12,14},{14,16},{16,18},{18... | collective-permute-start | bytes 3145736 | tf_op jit(solution)/shard_map/ppermute | solution.py:20
  97.6 3.3 fusion.69
  101.0 3.0 add_subtract_fusion.1
  108.4 16.2 %collective-permute-done.2 = f32[256,1024]{1,0:T(8,128)} collective-permute-done((f32[256,1024]{1,0:T(8,128)}, f32[256,1024]{1,0:T(8,128)}, u32[]{:S(2)}, u32[]{:S(2)}) %collective-permute-start.2) | collective-permute-done | bytes 1048608 | tf_op jit(solution)/shard_map/ppermute | solution.py:20
  124.6 3.3 fusion.24
  131.0 15.8 %collective-permute-done.3 = f32[256,1024]{1,0:T(8,128)} collective-permute-done((f32[256,1024]{1,0:T(8,128)}, f32[256,1024]{1,0:T(8,128)}, u32[]{:S(2)}, u32[]{:S(2)}) %collective-permute-start.3) | collective-permute-done | bytes 1048608 | tf_op jit(solution)/shard_map/ppermute | solution.py:20
  146.8 2.7 multiply_convert_fusion.9
  149.5 3.7 fusion.41
  154.6 13.2 %all-gather.13.cloned.1.call-done = bf16[512,1024]{1,0:T(8,128)(2,1)} async-done(((bf16[256,1024]{1,0:T(8,128)(2,1)}), bf16[512,1024]{1,0:T(8,128)(2,1)}) %all-gather.13.cloned.1.call-update) | async-done | bytes 1048592 | tf_op jit(solution)/shard_map/all_gather | solution.py:88
  167.8 23.4 %all-gather.15.cloned.1.call-done = bf16[512,1024]{1,0:T(8,128)(2,1)} async-done(((bf16[256,1024]{1,0:T(8,128)(2,1)}), bf16[512,1024]{1,0:T(8,128)(2,1)}) %all-gather.15.cloned.1.call-update) | async-done | bytes 1048592 | tf_op jit(solution)/shard_map/all_gather | solution.py:93
  191.2 3.4 multiply_bitcast_fusion.3
  194.6 19.9 %all-gather.17.cloned.1.call-done = bf16[512,1024]{1,0:T(8,128)(2,1)} async-done(((bf16[256,1024]{1,0:T(8,128)(2,1)}), bf16[512,1024]{1,0:T(8,128)(2,1)}) %all-gather.17.cloned.1.call-update) | async-done | bytes 1048592 | tf_op jit(solution)/shard_map/all_gather | solution.py:88
  214.5 23.3 %all-gather.19.cloned.1.call-done = bf16[512,1024]{1,0:T(8,128)(2,1)} async-done(((bf16[256,1024]{1,0:T(8,128)(2,1)}), bf16[512,1024]{1,0:T(8,128)(2,1)}) %all-gather.19.cloned.1.call-update) | async-done | bytes 1048592 | tf_op jit(solution)/shard_map/all_gather | solution.py:93
  241.4 5.8 %fusion = bf16[2,512,1024]{2,1,0:T(8,128)(2,1)} fusion(f32[2,512,1024]{2,1,0:T(8,128)S(1)} %copy-done.6, f32[1,512,1024]{2,1,0:T(8,128)S(1)} %multiply_bitcast_fusion.2, f32[1,512,1024]{2,1,0:T(8,128)} %multiply_bitcast_fusion.3, f32[2,512,1024]{2,1,0:T(8,128)} %param.6), kind=kLoop, calls=%fused_computation.12 | loop fusion | flops 6291456 | bytes 14680064 | tf_op jit(solution)/shard_map/convert_element_type | solution.py:70
  247.3 56.8 %all-gather.21.cloned.1.call-done = bf16[2,1024,1024]{2,1,0:T(8,128)(2,1)} async-done(((bf16[2,512,1024]{2,1,0:T(8,128)(2,1)}), bf16[2,1024,1024]{2,1,0:T(8,128)(2,1)}) %all-gather.21.cloned.1.call-update) | async-done | bytes 4194320 | tf_op jit(solution)/shard_map/all_gather | solution.py:70
  313.2 13.3 %collective-permute-start.5 = (f32[256,1024]{1,0:T(8,128)S(1)}, f32[256,1024]{1,0:T(8,128)S(1)}, u32[]{:S(2)}, u32[]{:S(2)}) collective-permute-start(f32[256,1024]{1,0:T(8,128)S(1)} %fusion.11), channel_id=1, source_target_pairs={{0,2},{2,4},{4,6},{6,8},{8,10},{10,12},{12,14},{14,16},{16,18},{18... | collective-permute-start | bytes 3145736 | tf_op jit(solution)/shard_map/ppermute | solution.py:20
  329.9 3.7 fusion.70
  333.6 3.3 add_subtract_fusion
  337.2 2.5 fusion.6
  341.7 14.7 %collective-permute-done.6 = f32[256,1024]{1,0:T(8,128)S(1)} collective-permute-done((f32[256,1024]{1,0:T(8,128)S(1)}, f32[256,1024]{1,0:T(8,128)S(1)}, u32[]{:S(2)}, u32[]{:S(2)}) %collective-permute-start.6) | collective-permute-done | bytes 1048608 | tf_op jit(solution)/shard_map/ppermute | solution.py:20
  360.4 15.8 %collective-permute-done.7 = f32[256,1024]{1,0:T(8,128)} collective-permute-done((f32[256,1024]{1,0:T(8,128)}, f32[256,1024]{1,0:T(8,128)}, u32[]{:S(2)}, u32[]{:S(2)}) %collective-permute-start.7) | collective-permute-done | bytes 1048608 | tf_op jit(solution)/shard_map/ppermute | solution.py:20
  376.3 2.7 fusion.71
  379.0 3.7 fusion.42
  384.1 13.1 %all-gather.23.cloned.1.call-done = bf16[512,1024]{1,0:T(8,128)(2,1)} async-done(((bf16[256,1024]{1,0:T(8,128)(2,1)}), bf16[512,1024]{1,0:T(8,128)(2,1)}) %all-gather.23.cloned.1.call-update) | async-done | bytes 1048592 | tf_op jit(solution)/shard_map/all_gather | solution.py:88
  397.2 22.9 %all-gather.25.cloned.1.call-done = bf16[512,1024]{1,0:T(8,128)(2,1)} async-done(((bf16[256,1024]{1,0:T(8,128)(2,1)}), bf16[512,1024]{1,0:T(8,128)(2,1)}) %all-gather.25.cloned.1.call-update) | async-done | bytes 1048592 | tf_op jit(solution)/shard_map/all_gather | solution.py:93
  420.1 3.5 multiply_bitcast_fusion.1
  423.5 19.4 %all-gather.27.cloned.1.call-done = bf16[512,1024]{1,0:T(8,128)(2,1)} async-done(((bf16[256,1024]{1,0:T(8,128)(2,1)}), bf16[512,1024]{1,0:T(8,128)(2,1)}) %all-gather.27.cloned.1.call-update) | async-done | bytes 1048592 | tf_op jit(solution)/shard_map/all_gather | solution.py:88
  442.9 23.3 %all-gather.29.cloned.1.call-done = bf16[512,1024]{1,0:T(8,128)(2,1)} async-done(((bf16[256,1024]{1,0:T(8,128)(2,1)}), bf16[512,1024]{1,0:T(8,128)(2,1)}) %all-gather.29.cloned.1.call-update) | async-done | bytes 1048592 | tf_op jit(solution)/shard_map/all_gather | solution.py:93
  468.9 6.5 %multiply_subtract_fusion = (f32[2,512,1024]{2,1,0:T(8,128)}, f32[2,512,1024]{2,1,0:T(8,128)}) fusion(f32[2,512,1024]{2,1,0:T(8,128)S(1)} %copy-done.7, f32[1,512,1024]{2,1,0:T(8,128)} %copy-done.13, f32[1,512,1024]{2,1,0:T(8,128)S(1)} %copy-done.12, f32[2,512,1024]{2,1,0:T(8,128)} %param.6, f32[1,512,1024]{2,1,0:T(8,128)S(1)} %multiply_bitcast_fusion, ...), kind=kLoop, calls=%fused_computation.2 | loop fusion | flops 10485760 | bytes 25165824 | tf_op jit(solution)/shard_map/sub | solution.py:100
  (85 shorter events, 46.0 us)
Async XLA Ops:
  7.2 63.6 %copy-start.16 = (f32[1,256,1024]{2,1,0:T(8,128)S(1)}, f32[1,256,1024]{2,1,0:T(8,128)}, u32[]{:S(2)}) copy-start(f32[1,256,1024]{2,1,0:T(8,128)} %param.7) | copy-start | bytes 3145732
  7.2 63.6 %all-gather.11.cloned.1.call-start = ((), (), s32[]{:S(2)}) async-start(), calls=%async_computation | async-start | bytes 6291456 | tf_op jit(solution)/shard_map/all_gather | solution.py:70
  11.2 156.6 %all-gather.13.cloned.1.call-start = ((), (), s32[]{:S(2)}) async-start(), calls=%async_computation.1 | async-start | bytes 1572864 | tf_op jit(solution)/shard_map/all_gather | solution.py:88
  74.3 3.9 collective-permute-start
  76.0 5.0 %copy-start.1 = (bf16[2,1024,1024]{2,1,0:T(8,128)(2,1)S(1)}, bf16[2,1024,1024]{2,1,0:T(8,128)(2,1)}, u32[]{:S(2)}) copy-start(bf16[2,1024,1024]{2,1,0:T(8,128)(2,1)} %all-gather.11.cloned.1.call-done) | copy-start | bytes 12582916
  78.2 3.6 copy-start.18
  81.7 15.5 %collective-permute-start.1 = (f32[256,1024]{1,0:T(8,128)S(1)}, f32[256,1024]{1,0:T(8,128)S(1)}, u32[]{:S(2)}, u32[]{:S(2)}) collective-permute-start(f32[256,1024]{1,0:T(8,128)S(1)} %fusion.31), channel_id=1, source_target_pairs={{0,2},{2,4},{4,6},{6,8},{8,10},{10,12},{12,14},{14,16},{16,18},{18... | collective-permute-start | bytes 3145736 | tf_op jit(solution)/shard_map/ppermute | solution.py:20
  97.6 3.3 copy-start.14
  101.0 3.3 copy-start.2
  101.0 3.6 copy-start.17
  107.1 17.6 %collective-permute-start.2 = (f32[256,1024]{1,0:T(8,128)}, f32[256,1024]{1,0:T(8,128)}, u32[]{:S(2)}, u32[]{:S(2)}) collective-permute-start(f32[256,1024]{1,0:T(8,128)} %fusion.25), channel_id=1, source_target_pairs={{2,0},{4,2},{6,4},{8,6},{10,8},{12,10},{14,12},{16,14},{18,16},{20... | collective-permute-start | bytes 3145736 | tf_op jit(solution)/shard_map/ppermute | solution.py:20
  108.4 19.5 %copy-start.3 = (bf16[2,1024,1024]{2,1,0:T(8,128)(2,1)S(1)}, bf16[2,1024,1024]{2,1,0:T(8,128)(2,1)}, u32[]{:S(2)}) copy-start(bf16[2,1024,1024]{2,1,0:T(8,128)(2,1)} %all-gather.11.cloned.1.call-done) | copy-start | bytes 12582916
  129.7 17.2 %collective-permute-start.3 = (f32[256,1024]{1,0:T(8,128)}, f32[256,1024]{1,0:T(8,128)}, u32[]{:S(2)}, u32[]{:S(2)}) collective-permute-start(f32[256,1024]{1,0:T(8,128)} %fusion.23), channel_id=1, source_target_pairs={{2,0},{4,2},{6,4},{8,6},{10,8},{12,10},{14,12},{16,14},{18,16},{20... | collective-permute-start | bytes 3145736 | tf_op jit(solution)/shard_map/ppermute | solution.py:20
  131.0 60.2 %all-gather.15.cloned.1.call-start = ((), (), s32[]{:S(2)}) async-start(), calls=%async_computation.2 | async-start | bytes 1572864 | tf_op jit(solution)/shard_map/all_gather | solution.py:93
  153.2 61.3 %all-gather.17.cloned.1.call-start = ((), (), s32[]{:S(2)}) async-start(), calls=%async_computation.3 | async-start | bytes 1572864 | tf_op jit(solution)/shard_map/all_gather | solution.py:88
  153.8 84.0 %all-gather.19.cloned.1.call-start = ((), (), s32[]{:S(2)}) async-start(), calls=%async_computation.4 | async-start | bytes 1572864 | tf_op jit(solution)/shard_map/all_gather | solution.py:93
  154.4 149.8 %all-gather.21.cloned.1.call-start = ((), (), s32[]{:S(2)}) async-start(), calls=%async_computation.5 | async-start | bytes 6291456 | tf_op jit(solution)/shard_map/all_gather | solution.py:70
  237.8 3.6 copy-start.6
  241.4 62.7 %copy-start.15 = (bf16[256,1024]{1,0:T(8,128)(2,1)S(1)}, bf16[256,1024]{1,0:T(8,128)(2,1)}, u32[]{:S(2)}) copy-start(bf16[256,1024]{1,0:T(8,128)(2,1)} %copy-done.14) | copy-start | bytes 1572868
  247.3 149.9 %all-gather.23.cloned.1.call-start = ((), (), s32[]{:S(2)}) async-start(), calls=%async_computation.6 | async-start | bytes 1572864 | tf_op jit(solution)/shard_map/all_gather | solution.py:88
  307.7 3.9 collective-permute-start.4
  313.2 15.6 %collective-permute-start.5 = (f32[256,1024]{1,0:T(8,128)S(1)}, f32[256,1024]{1,0:T(8,128)S(1)}, u32[]{:S(2)}, u32[]{:S(2)}) collective-permute-start(f32[256,1024]{1,0:T(8,128)S(1)} %fusion.11), channel_id=1, source_target_pairs={{0,2},{2,4},{4,6},{6,8},{8,10},{10,12},{12,14},{14,16},{16,18},{18... | collective-permute-start | bytes 3145736 | tf_op jit(solution)/shard_map/ppermute | solution.py:20
  329.9 3.7 copy-start.11
  333.6 3.6 copy-start.5
  336.9 19.6 %copy-start.8 = (f32[256,1024]{1,0:T(8,128)}, f32[256,1024]{1,0:T(8,128)S(1)}, u32[]{:S(2)}) copy-start(f32[256,1024]{1,0:T(8,128)S(1)} %get-tuple-element.19) | copy-start | bytes 3145732
  340.4 16.0 %collective-permute-start.6 = (f32[256,1024]{1,0:T(8,128)S(1)}, f32[256,1024]{1,0:T(8,128)S(1)}, u32[]{:S(2)}, u32[]{:S(2)}) collective-permute-start(f32[256,1024]{1,0:T(8,128)S(1)} %fusion.5), channel_id=1, source_target_pairs={{2,0},{4,2},{6,4},{8,6},{10,8},{12,10},{14,12},{16,14},{18,16},{20... | collective-permute-start | bytes 3145736 | tf_op jit(solution)/shard_map/ppermute | solution.py:20
  357.3 19.0 %copy-start.9 = (f32[256,1024]{1,0:T(8,128)S(1)}, f32[256,1024]{1,0:T(8,128)}, u32[]{:S(2)}) copy-start(f32[256,1024]{1,0:T(8,128)} %copy-done.8) | copy-start | bytes 3145732
  359.1 17.2 %collective-permute-start.7 = (f32[256,1024]{1,0:T(8,128)}, f32[256,1024]{1,0:T(8,128)}, u32[]{:S(2)}, u32[]{:S(2)}) collective-permute-start(f32[256,1024]{1,0:T(8,128)} %fusion.3), channel_id=1, source_target_pairs={{2,0},{4,2},{6,4},{8,6},{10,8},{12,10},{14,12},{16,14},{18,16},{20... | collective-permute-start | bytes 3145736 | tf_op jit(solution)/shard_map/ppermute | solution.py:20
  360.4 59.7 %all-gather.25.cloned.1.call-start = ((), (), s32[]{:S(2)}) async-start(), calls=%async_computation.7 | async-start | bytes 1572864 | tf_op jit(solution)/shard_map/all_gather | solution.py:93
  382.7 60.2 %all-gather.27.cloned.1.call-start = ((), (), s32[]{:S(2)}) async-start(), calls=%async_computation.8 | async-start | bytes 1572864 | tf_op jit(solution)/shard_map/all_gather | solution.py:88
  383.5 82.7 %all-gather.29.cloned.1.call-start = ((), (), s32[]{:S(2)}) async-start(), calls=%async_computation.9 | async-start | bytes 1572864 | tf_op jit(solution)/shard_map/all_gather | solution.py:93
  384.1 84.4 %copy-start.12 = (f32[1,512,1024]{2,1,0:T(8,128)S(1)}, f32[1,512,1024]{2,1,0:T(8,128)}, u32[]{:S(2)}) copy-start(f32[1,512,1024]{2,1,0:T(8,128)} %multiply_bitcast_fusion.3) | copy-start | bytes 6291460
  (5 other events, 12.8 us)
Sparse Core Ops, SparseCore 0:
  11.3 59.4 all-gather.10
  131.1 36.6 all-gather.12
  169.9 21.2 all-gather.14
  193.2 21.2 all-gather.16
  216.5 21.2 all-gather.18
  247.4 56.7 all-gather.20
  360.5 36.6 all-gather.22
  398.8 21.2 all-gather.24
  421.6 21.2 all-gather.26
  444.9 21.2 all-gather.28
where the time goes:
time: 483 us; the launch traced here: 482 us
  waiting for transfers between devices  348 us (72%)
  matrix products  57.1 us (12%)
  starting transfers between devices  35.9 us (7%)
  other arithmetic  23.1 us (5%)
  between operations  14.5 us (3%)
    all_gather x2, waiting for transfers between devices, local(): lax.all_gather(weights.astype(jnp.bfloat16), 'dp', axis=1, tiled=True)  116 us
    all_gather x4, waiting for transfers between devices, local(): lax.all_gather(signal, 'dp', axis=0, tiled=True)  92.9 us
    ppermute x8, waiting for transfers between devices, passed_along(): return lax.ppermute(value, axis, pairs)  71.4 us
    all_gather x4, waiting for transfers between devices, local(): lax.all_gather(layer_input, 'dp', axis=0, tiled=True)  65.5 us
    ppermute x8, starting transfers between devices, passed_along(): return lax.ppermute(value, axis, pairs)  35.1 us
    dot_general x12, matrix products, forward_group(): jnp.dot(rounded, full_weights[layer_at], preferred_element_type=jnp.float32)  24.8 us
    dot_general x10, matrix products, pull_back(): lax.dot_general(signal, matrix, (((1,), (1,)), ((), ())), preferred_eleme...  20.8 us
    dot_general x4, matrix products, outer_rows(): lax.dot_general(left, right, (((0,), (0,)), ((), ())), preferred_element_...  11.4 us
  transfers between devices with their start and end apart: 18, of which 18 were waited for; matrix products, arithmetic and copies ran while one was open for 4% of the time, Pallas kernels for 0%

commit v1 on v0

v1 whole, which is shorter than its diff:
```python
import functools
import math

import jax
import jax.numpy as jnp
from jax import lax
from jax.experimental import pallas as pl
from jax.experimental.pallas import tpu as pltpu
from jax.sharding import PartitionSpec as P

STEPS = 2
SWEEPS = 2

step_size = 0.5
momentum_decay = 0.9
learn_rate = 0.05

MESH = pl.DeviceIdType.MESH
f32 = jnp.float32
bf16 = jnp.bfloat16


def kernel(
    groups, shards,
    w_in, m_in, b_in, a_in, t_in,
    w_out, m_out, b_out, a_out,
    wst, mst, wfull, vfull, xcur, acur, tgt, xw, in0, slopes,
    xb, ab, mids, sigs, stage,
    load_sem, store_sem, w_send, w_recv, v_send, v_recv,
    hop_send, hop_recv, ex_send, ex_recv,
):
    layers, own, width = wst.shape
    rows = xcur.shape[0]
    tile = min(256, width)
    tiles = width // tile
    g = lax.axis_index("layer")
    me = lax.axis_index("dp")
    is_first = g == 0
    is_last = g == groups - 1
    not_first = g > 0
    not_last = g < groups - 1
    width_scale = 1.0 / math.sqrt(width)
    row_scale = 1.0 / math.sqrt(rows * shards)

    def peer(d):
        return lax.rem(me + d, shards)

    def source(d):
        return lax.rem(me + shards - d, shards)

    loads = []
    for l in range(layers):
        loads.append(pltpu.make_async_copy(w_in.at[l], wst.at[l], load_sem.at[l]))
    loads.append(pltpu.make_async_copy(b_in.at[0], xcur, load_sem.at[layers]))
    loads.append(pltpu.make_async_copy(m_in, mst, load_sem.at[layers + 1]))
    loads.append(pltpu.make_async_copy(a_in.at[0], acur, load_sem.at[layers + 2]))
    loads.append(pltpu.make_async_copy(t_in, tgt, load_sem.at[layers + 3]))
    for c in loads:
        c.start()

    barrier = pltpu.get_barrier_semaphore()

    @pl.when(not_first)
    def _():
        pl.semaphore_signal(barrier, inc=1, device_id={"layer": g - 1}, device_id_type=MESH)

    @pl.when(not_last)
    def _():
        pl.semaphore_signal(barrier, inc=1, device_id={"layer": g + 1}, device_id_type=MESH)

    for d in range(1, shards):
        pl.semaphore_signal(barrier, inc=1, device_id={"dp": peer(d)}, device_id_type=MESH)

    own_rows = pl.ds(pl.multiple_of(me * own, own), own)

    def block_copy(buf, l, d, sends, recvs, sender):
        region = buf.at[l, pl.ds(pl.multiple_of(sender * own, own), own)]
        return pltpu.make_async_remote_copy(
            src_ref=region, dst_ref=region,
            send_sem=sends.at[l, d - 1], recv_sem=recvs.at[l, d - 1],
            device_id={"dp": peer(d)}, device_id_type=MESH,
        )

    neighbours = not_first.astype(jnp.int32) + not_last.astype(jnp.int32) + (shards - 1)
    for l in range(layers):
        loads[l].wait()
        wfull[l, own_rows, :] = wst[l].astype(bf16)
        if l == 0:
            pl.semaphore_wait(barrier, neighbours)
        for d in range(1, shards):
            block_copy(wfull, l, d, w_send, w_recv, me).start()
    loads[layers + 1].wait()
    for l in range(layers):
        vfull[l, own_rows, :] = (wst[l] - learn_rate * momentum_decay * mst[l]).astype(bf16)
        for d in range(1, shards):
            block_copy(vfull, l, d, v_send, v_recv, me).start()
    for c in loads[layers:layers + 1] + loads[layers + 2:]:
        c.wait()

    def columns(j, n=tile):
        return pl.ds(pl.multiple_of(j * n, n), n)

    def hop(t, way, s, j):
        slot = jnp.where(s == SWEEPS - 1, me, shards)
        into = (xb, ab)[way]
        return pltpu.make_async_remote_copy(
            src_ref=stage.at[way, s, :, columns(j)],
            dst_ref=into.at[t, slot, :, columns(j)],
            send_sem=hop_send.at[t, way, s, j], recv_sem=hop_recv.at[t, way, s, j],
            device_id={"layer": g + 1 if way == 0 else g - 1}, device_id_type=MESH,
        )

    def exchange(t, way, d, sender):
        into = (xb, ab)[way]
        return pltpu.make_async_remote_copy(
            src_ref=into.at[t, sender], dst_ref=into.at[t, sender],
            send_sem=ex_send.at[t, way, d - 1], recv_sem=ex_recv.at[t, way, d - 1],
            device_id={"dp": peer(d)}, device_id_type=MESH,
        )

    def forward(first_x, keep, emit):
        for l in range(layers):
            last = l == layers - 1
            source_ref = in0 if l == 0 else keep.at[l - 1]

            @pl.loop(0, tiles)
            def _(j):
                cols = columns(j)
                product = jnp.dot(source_ref[...], wfull[l, :, cols], preferred_element_type=f32)
                squashed = jnp.tanh(product * width_scale)
                slopes[l, :, cols] = squashed
                before = first_x(cols) if l == 0 else xw[:, cols]
                after = before + step_size * squashed
                if last:
                    if emit is not None:
                        emit(j, cols, after)
                else:
                    xw[:, cols] = after
                    keep[l, :, cols] = after.astype(bf16)

    def backward(first_a, keep, emit):
        for l in reversed(range(layers)):
            start = first_a if l == layers - 1 else (lambda cols: xw[:, cols])

            @pl.loop(0, tiles)
            def _(j):
                cols = columns(j)
                slope = slopes[l, :, cols]
                keep[l, :, cols] = (start(cols) * (1.0 - slope * slope)).astype(bf16)

            if l == 0 and emit is None:
                continue

            @pl.loop(0, tiles)
            def _(j):
                cols = columns(j)
                pulled = lax.dot_general(
                    keep[l], wfull[l, cols, :], (((1,), (1,)), ((), ())),
                    preferred_element_type=f32,
                )
                after = start(cols) + (step_size * width_scale) * pulled
                if l == 0:
                    emit(j, cols, after)
                else:
                    xw[:, cols] = after

    def own_x(cols):
        return xcur[:, cols]

    def own_a(cols):
        return acur[:, cols]

    for t in range(STEPS):
        own_mids = mids.at[me]
        own_sigs = sigs.at[me]
        if t == 0:
            for l in range(layers):
                for d in range(1, shards):
                    block_copy(wfull, l, d, w_send, w_recv, source(d)).wait_recv()

        @pl.when(is_first)
        def _():
            xb[t, me] = xcur[...].astype(bf16)

        @pl.loop(0, SWEEPS)
        def _(s):
            in0[...] = xcur[...].astype(bf16)

            def emit(j, cols, after):
                stage[0, s, :, cols] = after.astype(bf16)

                @pl.when(not_last)
                def _():
                    hop(t, 0, s, j).start()

            forward(own_x, own_mids, emit)

            @pl.when(not_first)
            def _():
                @pl.loop(0, tiles)
                def _(j):
                    hop(t, 0, s, j).wait_recv()

                slot = jnp.where(s == SWEEPS - 1, me, shards)
                xcur[...] = xb[t, slot].astype(f32)

        for d in range(1, shards):
            exchange(t, 0, d, me).start()
        if t == STEPS - 1:
            b_store = pltpu.make_async_copy(xcur, b_out.at[0], store_sem.at[0])
            b_store.start()
        in0[...] = xcur[...].astype(bf16)

        def finals(j, cols, after):
            @pl.when(is_last)
            def _():
                ab[t, me, :, cols] = (after - tgt[:, cols]).astype(bf16)

        forward(own_x, own_mids, finals)

        @pl.loop(0, SWEEPS)
        def _(s):
            def emit(j, cols, after):
                stage[1, s, :, cols] = after.astype(bf16)

                @pl.when(not_first)
                def _():
                    hop(t, 1, s, j).start()

            backward(own_a, own_sigs, emit)

            @pl.when(not_last)
            def _():
                @pl.loop(0, tiles)
                def _(j):
                    hop(t, 1, s, j).wait_recv()

                slot = jnp.where(s == SWEEPS - 1, me, shards)
                acur[...] = ab[t, slot].astype(f32)

            @pl.when(is_last)
            def _():
                acur[...] = ab[t, me].astype(f32)

        for d in range(1, shards):
            exchange(t, 1, d, me).start()
        if t == STEPS - 1:
            a_store = pltpu.make_async_copy(acur, a_out.at[0], store_sem.at[1])
            a_store.start()
        backward(own_a, own_sigs, None)

        @pl.loop(1, shards)
        def _(d):
            s = source(d)
            exchange(t, 0, d, s).wait_recv()
            in0[...] = xb[t, s]
            forward(lambda cols: xb[t, s, :, cols].astype(f32), mids.at[s], None)
            exchange(t, 1, d, s).wait_recv()
            backward(lambda cols: ab[t, s, :, cols].astype(f32), sigs.at[s], None)

        if t == 0:
            for l in range(layers):
                for d in range(1, shards):
                    block_copy(vfull, l, d, v_send, v_recv, source(d)).wait_recv()
                    block_copy(wfull, l, d, w_send, w_recv, me).wait_send()

        part = min(256, own)
        wide = min(512, width)

        def gradient(l, at, j):
            feats = pl.ds(pl.multiple_of(at, part), part)
            if l == 0:
                left = xb[t, 0:shards, :, feats].reshape(shards * rows, part)
            else:
                left = mids[:, l - 1, :, feats].reshape(shards * rows, part)
            right = sigs[:, l, :, columns(j, wide)].reshape(shards * rows, wide)
            return lax.dot_general(
                left, right, (((0,), (0,)), ((), ())), preferred_element_type=f32
            ) * row_scale

        for l in range(layers):
            @pl.loop(0, own // part)
            def _(i):
                @pl.loop(0, width // wide)
                def _(j):
                    cols = columns(j, wide)
                    here = pl.ds(pl.multiple_of(i * part, part), part)
                    at = me * own + i * part
                    moved = momentum_decay * mst[l, here, cols] + gradient(l, at, j)
                    mst[l, here, cols] = moved
                    fresh = wst[l, here, cols] - learn_rate * moved
                    wst[l, here, cols] = fresh
                    if t < STEPS - 1:
                        there = pl.ds(pl.multiple_of(at, part), part)
                        wfull[l, there, cols] = fresh.astype(bf16)

            if t < STEPS - 1:
                @pl.loop(1, shards)
                def _(d):
                    @pl.loop(0, own // part)
                    def _(i):
                        @pl.loop(0, width // wide)
                        def _(j):
                            cols = columns(j, wide)
                            at = source(d) * own + i * part
                            there = pl.ds(pl.multiple_of(at, part), part)
                            fresh = vfull[l, there, cols].astype(f32) - learn_rate * gradient(l, at, j)
                            wfull[l, there, cols] = fresh.astype(bf16)

        if t == STEPS - 1:
            w_store = pltpu.make_async_copy(wst, w_out, store_sem.at[2])
            m_store = pltpu.make_async_copy(mst, m_out, store_sem.at[3])
            w_store.start()
            m_store.start()

        @pl.loop(0, SWEEPS)
        def _(s):
            @pl.loop(0, tiles)
            def _(j):
                @pl.when(not_last)
                def _():
                    hop(t, 0, s, j).wait_send()

                @pl.when(not_first)
                def _():
                    hop(t, 1, s, j).wait_send()

        for d in range(1, shards):
            exchange(t, 0, d, me).wait_send()
            exchange(t, 1, d, me).wait_send()
            if t == 0:
                for l in range(layers):
                    block_copy(vfull, l, d, v_send, v_recv, me).wait_send()

    for c in (b_store, a_store, w_store, m_store):
        c.wait()


def local(groups, shards, weights, momentum, boundary, adjoint, target):
    layers, own, width = weights.shape
    rows = target.shape[0]
    tiles = width // min(256, width)
    others = max(shards - 1, 1)
    dma = pltpu.SemaphoreType.DMA
    anywhere = pl.BlockSpec(memory_space=pl.ANY)
    return pl.pallas_call(
        functools.partial(kernel, groups, shards),
        out_shape=tuple(
            jax.ShapeDtypeStruct(v.shape, f32) for v in (weights, momentum, boundary, adjoint)
        ),
        in_specs=[anywhere] * 5,
        out_specs=(anywhere,) * 4,
        scratch_shapes=[
            pltpu.VMEM((layers, own, width), f32),
            pltpu.VMEM((layers, own, width), f32),
            pltpu.VMEM((layers, width, width), bf16),
            pltpu.VMEM((layers, width, width), bf16),
            pltpu.VMEM((rows, width), f32),
            pltpu.VMEM((rows, width), f32),
            pltpu.VMEM((rows, width), f32),
            pltpu.VMEM((rows, width), f32),
            pltpu.VMEM((rows, width), bf16),
            pltpu.VMEM((layers, rows, width), f32),
            pltpu.VMEM((STEPS, shards + 1, rows, width), bf16),
            pltpu.VMEM((STEPS, shards + 1, rows, width), bf16),
            pltpu.VMEM((shards, max(layers - 1, 1), rows, width), bf16),
            pltpu.VMEM((shards, layers, rows, width), bf16),
            pltpu.VMEM((2, SWEEPS, rows, width), bf16),
            dma((layers + 4,)),
            dma((4,)),
            dma((layers, others)),
            dma((layers, others)),
            dma((layers, others)),
            dma((layers, others)),
            dma((STEPS, 2, SWEEPS, tiles)),
            dma((STEPS, 2, SWEEPS, tiles)),
            dma((STEPS, 2, others)),
            dma((STEPS, 2, others)),
        ],
        compiler_params=pltpu.CompilerParams(
            collective_id=0, has_side_effects=True, vmem_limit_bytes=63 * 1024 * 1024
        ),
    )(weights, momentum, boundary, adjoint, target)


def solution(mesh):
    placed = P("layer", "dp", None)
    return jax.shard_map(
        functools.partial(local, mesh.shape["layer"], mesh.shape["dp"]),
        mesh=mesh,
        in_specs=(placed,) * 4 + (P("dp", None),),
        out_specs=(placed,) * 4,
        check_vma=False,
    )
```

time: 483 us -> 188 us (0.39)
  waiting for transfers between devices: 348 us -> 0 us
  Pallas kernels: 0 us -> 177 us
  matrix products: 57.1 us -> 0 us
  starting transfers between devices: 35.9 us -> 0 us
  other arithmetic: 23.1 us -> 0 us
  between operations: 14.5 us -> 0.65 us
  local copies, waits for them, and re-layouts: 3.36 us -> 9.02 us
    all_gather x10 -> x0, waiting for transfers between devices: 275 us -> none  [the longest x2 116 us: local(): lax.all_gather(weights.astype(jnp.bfloat16), 'dp', axis=1, tiled=True)]
    pallas_call x0 -> x1, Pallas kernels: none -> 177 us  [local(): pl.pallas_call(functools.partial(kernel, groups, shards), out_shape=tuple...]
    ppermute x8 -> x0, waiting for transfers between devices: 71.4 us -> none  [passed_along(): return lax.ppermute(value, axis, pairs)]
    dot_general x26 -> x0, matrix products: 57.1 us -> none  [the longest x12 24.8 us: forward_group(): jnp.dot(rounded, full_weights[layer_at], preferred_element_type=jnp.float32)]
    ppermute x8 -> x0, starting transfers between devices: 35.1 us -> none  [passed_along(): return lax.ppermute(value, axis, pairs)]
    convert_element_type x5 -> x0, other arithmetic: 13.8 us -> none  [the longest x2 9.74 us: local(): weights.astype(jnp.bfloat16)]
    sub x1 -> x0, other arithmetic: 6.52 us -> none  [local(): weights = weights - learn_rate * momentum]
    unnamed x38 -> x10, local copies, waits for them, and re-layouts: 3.36 us -> 9.02 us
  transfers between devices with their start and end apart: 18 -> 0, of which waited for: 18 -> 0; matrix products, arithmetic and copies ran while one was open for 4% -> 0% of each run, Pallas kernels for 0% -> 0%
where the time goes in v1:
time: 188 us; the launch traced here: 187 us
  Pallas kernels  177 us (94%)
  local copies, waits for them, and re-layouts  9.02 us (5%)
    pallas_call x1, Pallas kernels, local(): pl.pallas_call(functools.partial(kernel, groups, shards), out_shape=tuple...  177 us
    unnamed x10, local copies, waits for them, and re-layouts  9.02 us

profile of v1, /device:TPU:0, one launch (start us, length us, event | category | flops | bytes accessed | tf_op | source)
XLA Modules:
  0.0 187.1 jit_solution(9795551047261283217)
XLA Ops:
  0.6 177.4 %shard_map.84 = (f32[2,512,1024]{2,1,0:T(8,128)}, f32[2,512,1024]{2,1,0:T(8,128)}, f32[1,256,1024]{2,1,0:T(8,128)}, f32[1,256,1024]{2,1,0:T(8,128)}) custom-call(f32[2,512,1024]{2,1,0:T(8,128)} %w_in.1, f32[2,512,1024]{2,1,0:T(8,128)} %m_in.1, f32[1,256,1024]{2,1,0:T(8,128)} %b_in.1, f32[1,256,1024]{2,1,0:T(8,128)} %a_in.1, f32[256,1024]{1,0:T(8,128)} %t_in.1), custom_call_target="tpu_custom_call" | custom-call | tf_op jit(solution)/shard_map/pallas_call | solution.py:346
  178.0 0.0 copy-start
  178.0 4.9 %copy.13 = f32[2,512,1024]{2,1,0:T(8,128)} copy(f32[2,512,1024]{2,1,0:T(8,128)} %get-tuple-element.8) | data formatting | bytes 8388608
  183.0 0.0 copy-done
  183.0 0.0 copy-start.2
  183.0 0.0 copy-start.1
  183.0 2.1 %copy.14 = f32[2,512,1024]{2,1,0:T(8,128)} copy(f32[2,512,1024]{2,1,0:T(8,128)S(1)} %copy-done) | data formatting | bytes 8388608
  185.1 0.0 copy-done.2
  185.1 1.0 copy.15
  186.1 0.0 copy-done.1
  186.1 1.0 copy.16
Async XLA Ops:
  178.0 5.0 %copy-start = (f32[2,512,1024]{2,1,0:T(8,128)S(1)}, f32[2,512,1024]{2,1,0:T(8,128)}, u32[]{:S(2)}) copy-start(f32[2,512,1024]{2,1,0:T(8,128)} %get-tuple-element.9) | copy-start | bytes 12582916
  183.0 2.1 %copy-start.2 = (f32[1,256,1024]{2,1,0:T(8,128)S(1)}, f32[1,256,1024]{2,1,0:T(8,128)}, u32[]{:S(2)}) copy-start(f32[1,256,1024]{2,1,0:T(8,128)} %get-tuple-element.10) | copy-start | bytes 3145732
  183.0 3.1 %copy-start.1 = (f32[1,256,1024]{2,1,0:T(8,128)S(1)}, f32[1,256,1024]{2,1,0:T(8,128)}, u32[]{:S(2)}) copy-start(f32[1,256,1024]{2,1,0:T(8,128)} %get-tuple-element.11) | copy-start | bytes 3145732

commit v2 on v1

--- a/solution.py
+++ b/solution.py
@@ -89,11 +89,16 @@
             pl.semaphore_wait(barrier, neighbours)
         for d in range(1, shards):
             block_copy(wfull, l, d, w_send, w_recv, me).start()
+    def send_v(of):
+        for l in of:
+            for d in range(1, shards):
+                block_copy(vfull, l, d, v_send, v_recv, me).start()
+
     loads[layers + 1].wait()
     for l in range(layers):
         vfull[l, own_rows, :] = (wst[l] - learn_rate * momentum_decay * mst[l]).astype(bf16)
-        for d in range(1, shards):
-            block_copy(vfull, l, d, v_send, v_recv, me).start()
+    spare = range(layers // 2, layers)
+    send_v(range(layers // 2))
     for c in loads[layers:layers + 1] + loads[layers + 2:]:
         c.wait()
 
@@ -110,22 +115,42 @@
             device_id={"layer": g + 1 if way == 0 else g - 1}, device_id_type=MESH,
         )
 
-    def exchange(t, way, d, sender):
+    def exchange(t, way, d, sender, j):
         into = (xb, ab)[way]
+        region = into.at[t, sender, :, columns(j)]
         return pltpu.make_async_remote_copy(
-            src_ref=into.at[t, sender], dst_ref=into.at[t, sender],
-            send_sem=ex_send.at[t, way, d - 1], recv_sem=ex_recv.at[t, way, d - 1],
+            src_ref=region, dst_ref=region,
+            send_sem=ex_send.at[t, way, d - 1, j], recv_sem=ex_recv.at[t, way, d - 1, j],
             device_id={"dp": peer(d)}, device_id_type=MESH,
         )
+
+    def receive(t, way, s, expects):
+        @pl.loop(0, tiles)
+        def _(j):
+            @pl.when(expects)
+            def _():
+                hop(t, way, s, j).wait_recv()
+
+            @pl.when(s == SWEEPS - 1)
+            def _():
+                for d in range(1, shards):
+                    exchange(t, way, d, me, j).start()
+
+    def arrive(t, way, d, s):
+        @pl.loop(0, tiles)
+        def _(j):
+            exchange(t, way, d, s, j).wait_recv()
 
     def forward(first_x, keep, emit):
         for l in range(layers):
             last = l == layers - 1
             source_ref = in0 if l == 0 else keep.at[l - 1]
 
-            @pl.loop(0, tiles)
+            size = tile if last and emit is not None else width
+
+            @pl.loop(0, width // size, unroll=True)
             def _(j):
-                cols = columns(j)
+                cols = columns(j, size)
                 product = jnp.dot(source_ref[...], wfull[l, :, cols], preferred_element_type=f32)
                 squashed = jnp.tanh(product * width_scale)
                 slopes[l, :, cols] = squashed
@@ -142,18 +167,18 @@
         for l in reversed(range(layers)):
             start = first_a if l == layers - 1 else (lambda cols: xw[:, cols])
 
-            @pl.loop(0, tiles)
-            def _(j):
-                cols = columns(j)
-                slope = slopes[l, :, cols]
-                keep[l, :, cols] = (start(cols) * (1.0 - slope * slope)).astype(bf16)
+            every = pl.ds(0, width)
+            slope = slopes[l]
+            keep[l] = (start(every) * (1.0 - slope * slope)).astype(bf16)
 
             if l == 0 and emit is None:
                 continue
 
-            @pl.loop(0, tiles)
+            size = tile if l == 0 else width
+
+            @pl.loop(0, width // size, unroll=True)
             def _(j):
-                cols = columns(j)
+                cols = columns(j, size)
                 pulled = lax.dot_general(
                     keep[l], wfull[l, cols, :], (((1,), (1,)), ((), ())),
                     preferred_element_type=f32,
@@ -195,17 +220,13 @@
 
             forward(own_x, own_mids, emit)
 
+            receive(t, 0, s, not_first)
+
             @pl.when(not_first)
             def _():
-                @pl.loop(0, tiles)
-                def _(j):
-                    hop(t, 0, s, j).wait_recv()
-
                 slot = jnp.where(s == SWEEPS - 1, me, shards)
                 xcur[...] = xb[t, slot].astype(f32)
 
-        for d in range(1, shards):
-            exchange(t, 0, d, me).start()
         if t == STEPS - 1:
             b_store = pltpu.make_async_copy(xcur, b_out.at[0], store_sem.at[0])
             b_store.start()
@@ -229,12 +250,10 @@
 
             backward(own_a, own_sigs, emit)
 
+            receive(t, 1, s, not_last)
+
             @pl.when(not_last)
             def _():
-                @pl.loop(0, tiles)
-                def _(j):
-                    hop(t, 1, s, j).wait_recv()
-
                 slot = jnp.where(s == SWEEPS - 1, me, shards)
                 acur[...] = ab[t, slot].astype(f32)
 
@@ -242,8 +261,8 @@
             def _():
                 acur[...] = ab[t, me].astype(f32)
 
-        for d in range(1, shards):
-            exchange(t, 1, d, me).start()
+        if t == 0:
+            send_v(spare)
         if t == STEPS - 1:
             a_store = pltpu.make_async_copy(acur, a_out.at[0], store_sem.at[1])
             a_store.start()
@@ -252,20 +271,19 @@
         @pl.loop(1, shards)
         def _(d):
             s = source(d)
-            exchange(t, 0, d, s).wait_recv()
+            arrive(t, 0, d, s)
             in0[...] = xb[t, s]
             forward(lambda cols: xb[t, s, :, cols].astype(f32), mids.at[s], None)
-            exchange(t, 1, d, s).wait_recv()
+            arrive(t, 1, d, s)
             backward(lambda cols: ab[t, s, :, cols].astype(f32), sigs.at[s], None)
 
         if t == 0:
             for l in range(layers):
                 for d in range(1, shards):
-                    block_copy(vfull, l, d, v_send, v_recv, source(d)).wait_recv()
                     block_copy(wfull, l, d, w_send, w_recv, me).wait_send()
 
-        part = min(256, own)
-        wide = min(512, width)
+        part = min(512, own)
+        wide = width
 
         def gradient(l, at, j):
             feats = pl.ds(pl.multiple_of(at, part), part)
@@ -294,18 +312,20 @@
                         there = pl.ds(pl.multiple_of(at, part), part)
                         wfull[l, there, cols] = fresh.astype(bf16)
 
-            if t < STEPS - 1:
-                @pl.loop(1, shards)
-                def _(d):
-                    @pl.loop(0, own // part)
-                    def _(i):
-                        @pl.loop(0, width // wide)
-                        def _(j):
-                            cols = columns(j, wide)
-                            at = source(d) * own + i * part
-                            there = pl.ds(pl.multiple_of(at, part), part)
-                            fresh = vfull[l, there, cols].astype(f32) - learn_rate * gradient(l, at, j)
-                            wfull[l, there, cols] = fresh.astype(bf16)
+        for l in range(layers if t < STEPS - 1 else 0):
+            @pl.loop(1, shards)
+            def _(d):
+                block_copy(vfull, l, d, v_send, v_recv, source(d)).wait_recv()
+
+                @pl.loop(0, own // part)
+                def _(i):
+                    @pl.loop(0, width // wide)
+                    def _(j):
+                        cols = columns(j, wide)
+                        at = source(d) * own + i * part
+                        there = pl.ds(pl.multiple_of(at, part), part)
+                        fresh = vfull[l, there, cols].astype(f32) - learn_rate * gradient(l, at, j)
+                        wfull[l, there, cols] = fresh.astype(bf16)
 
         if t == STEPS - 1:
             w_store = pltpu.make_async_copy(wst, w_out, store_sem.at[2])
@@ -326,8 +346,11 @@
                     hop(t, 1, s, j).wait_send()
 
         for d in range(1, shards):
-            exchange(t, 0, d, me).wait_send()
-            exchange(t, 1, d, me).wait_send()
+            @pl.loop(0, tiles)
+            def _(j):
+                exchange(t, 0, d, me, j).wait_send()
+                exchange(t, 1, d, me, j).wait_send()
+
             if t == 0:
                 for l in range(layers):
                     block_copy(vfull, l, d, v_send, v_recv, me).wait_send()
@@ -374,8 +397,8 @@
             dma((layers, others)),
             dma((STEPS, 2, SWEEPS, tiles)),
             dma((STEPS, 2, SWEEPS, tiles)),
-            dma((STEPS, 2, others)),
-            dma((STEPS, 2, others)),
+            dma((STEPS, 2, others, tiles)),
+            dma((STEPS, 2, others, tiles)),
         ],
         compiler_params=pltpu.CompilerParams(
             collective_id=0, has_side_effects=True, vmem_limit_bytes=63 * 1024 * 1024

time: 188 us -> 176 us (0.936)
  Pallas kernels: 177 us -> 166 us
    pallas_call x1, Pallas kernels: 177 us -> 166 us  [local(): pl.pallas_call(functools.partial(kernel, groups, shards), out_shape=tuple...]
where the time goes in v2:
time: 176 us; the launch traced here: 175 us
  Pallas kernels  166 us (94%)
  local copies, waits for them, and re-layouts  9.02 us (5%)
    pallas_call x1, Pallas kernels, local(): pl.pallas_call(functools.partial(kernel, groups, shards), out_shape=tuple...  166 us
    unnamed x10, local copies, waits for them, and re-layouts  9.02 us

profile of v2, /device:TPU:0, one launch (start us, length us, event | category | flops | bytes accessed | tf_op | source)
XLA Modules:
  0.0 175.4 jit_solution(12710713984925261884)
XLA Ops:
  0.6 165.7 %shard_map.84 = (f32[2,512,1024]{2,1,0:T(8,128)}, f32[2,512,1024]{2,1,0:T(8,128)}, f32[1,256,1024]{2,1,0:T(8,128)}, f32[1,256,1024]{2,1,0:T(8,128)}) custom-call(f32[2,512,1024]{2,1,0:T(8,128)} %w_in.1, f32[2,512,1024]{2,1,0:T(8,128)} %m_in.1, f32[1,256,1024]{2,1,0:T(8,128)} %b_in.1, f32[1,256,1024]{2,1,0:T(8,128)} %a_in.1, f32[256,1024]{1,0:T(8,128)} %t_in.1), custom_call_target="tpu_custom_call" | custom-call | tf_op jit(solution)/shard_map/pallas_call | solution.py:369
  166.4 0.0 copy-start
  166.4 4.9 %copy.13 = f32[2,512,1024]{2,1,0:T(8,128)} copy(f32[2,512,1024]{2,1,0:T(8,128)} %get-tuple-element.8) | data formatting | bytes 8388608
  171.3 0.0 copy-done
  171.3 0.0 copy-start.2
  171.3 0.0 copy-start.1
  171.3 2.1 %copy.14 = f32[2,512,1024]{2,1,0:T(8,128)} copy(f32[2,512,1024]{2,1,0:T(8,128)S(1)} %copy-done) | data formatting | bytes 8388608
  173.5 0.0 copy-done.2
  173.5 1.0 copy.15
  174.4 0.0 copy-done.1
  174.4 1.0 copy.16
Async XLA Ops:
  166.4 5.0 %copy-start = (f32[2,512,1024]{2,1,0:T(8,128)S(1)}, f32[2,512,1024]{2,1,0:T(8,128)}, u32[]{:S(2)}) copy-start(f32[2,512,1024]{2,1,0:T(8,128)} %get-tuple-element.9) | copy-start | bytes 12582916
  171.3 2.1 %copy-start.2 = (f32[1,256,1024]{2,1,0:T(8,128)S(1)}, f32[1,256,1024]{2,1,0:T(8,128)}, u32[]{:S(2)}) copy-start(f32[1,256,1024]{2,1,0:T(8,128)} %get-tuple-element.10) | copy-start | bytes 3145732
  171.3 3.1 %copy-start.1 = (f32[1,256,1024]{2,1,0:T(8,128)S(1)}, f32[1,256,1024]{2,1,0:T(8,128)}, u32[]{:S(2)}) copy-start(f32[1,256,1024]{2,1,0:T(8,128)} %get-tuple-element.11) | copy-start | bytes 3145732
